TPU v7x, 32 devices: a whole 2x2x4 slice. The times are simulated.
32 devices in a mesh: section: 2 (over y), blk: 8 (over z, x), mp: 2 (over core).
Axes of the slice: x: 2, y: 2, z: 4, core: 2. Of those that a mesh axis runs over, the one named last changes fastest.
Arguments:
- queries: bfloat16 [2, 1024, 4096], P('section', 'blk', 'mp'), may hold values from -210 to 210
- encoder_states: bfloat16 [512, 2048], P(('blk', 'section', 'mp')), may hold values from -200 to 200
- norm_gain: float32 [2048], replicated, may hold values from 0.25 to 1.75
- kv_weight: bfloat16 [2, 2048, 2, 512], P('section', 'blk', None, 'mp'), may hold values from -0.125 to 0.125
- span_len: int32 [64], replicated, may hold values from 1 to 57, as said below
- span_owner: int32 [64], replicated, may hold values from 0 to 7, as said below
Outputs:
- attended: bfloat16 [2, 1024, 4096], P('section', 'blk', 'mp')
Inputs may be any that keep to these rules, and one draw needn't show every extreme that they name: `span_owner`: each span lies whole in the slots of one blk index; each blk index owns exactly 8 spans. `span_len`: the spans of one blk index hold at most 64 tokens together, exactly 64 for some blk index in every draw; all spans hold 288 tokens together; one span holds exactly 57 tokens in every draw.
All inputs are finite; a program needn't handle non-finite values.
Results may differ from a plain program's by a relative error of at most 0.0094.
Values may be sent and summed in bfloat16 or wider, within the bound.
No kernel may reach another device: no remote copies, remote signals or barrier semaphores. Data moves between devices by JAX's collectives and lax.ppermute only.
A program may use at most 64 MiB of HBM per device.

v0:
```python
import jax
import jax.numpy as jnp
from jax import lax
from jax.sharding import PartitionSpec as P

HEADS = 32
KVH = 4
HD = 128


def normalize(states, norm_gain):
    widened = states.astype(jnp.float32)
    factor = lax.rsqrt(jnp.mean(widened * widened, axis=-1, keepdims=True) + 1e-05)
    return (widened * factor * norm_gain).astype(jnp.bfloat16)


def slot_loads(span_len, span_owner, block_count):
    owners = span_owner[:, None] == jnp.arange(block_count, dtype=jnp.int32)[None, :]
    return jnp.sum(jnp.where(owners, span_len[:, None], 0), axis=0)


def live_slots(slot_load, row_count, capacity):
    slot_ids = jnp.arange(row_count, dtype=jnp.int32)
    holder = slot_ids // capacity
    picked = holder[:, None] == jnp.arange(slot_load.shape[0], dtype=jnp.int32)[None, :]
    holder_load = jnp.sum(jnp.where(picked, slot_load[None, :], 0), axis=1)
    return slot_ids % capacity < holder_load


def attend_block(state_now, query_grid, key_rows, value_rows, alive):
    running_max, denominator, numerator = state_now
    row_count = key_rows.shape[0]
    groups = query_grid.shape[1]
    head_size = query_grid.shape[3]
    key_grid = key_rows.reshape(row_count, groups, head_size)
    value_grid = value_rows.reshape(row_count, groups, head_size)
    scores = jnp.einsum(
        "qgjd,rgd->qgjr", query_grid, key_grid, preferred_element_type=jnp.float32
    ) * head_size ** (-0.5)
    scores = jnp.where(alive, scores, -1e30)
    new_max = jnp.maximum(running_max, jnp.max(scores, axis=-1))
    weights = jnp.where(alive, jnp.exp(scores - new_max[..., None]), 0.0)
    denominator = jnp.sum(weights, axis=-1)
    numerator = jnp.einsum(
        "qgjr,rgd->qgjd",
        weights.astype(jnp.bfloat16),
        value_grid,
        preferred_element_type=jnp.float32,
    )
    return (new_max, denominator, numerator)


def attend(state_now, query_grid, key_rows, value_rows, slot_load, capacity):
    row_count = key_rows.shape[0]
    alive = live_slots(slot_load, row_count, capacity)
    return attend_block(state_now, query_grid, key_rows, value_rows, alive)


def local(queries, encoder_states, norm_gain, kv_weight, span_len, span_owner):
    gathered = lax.all_gather(encoder_states, ("section", "mp"), axis=0, tiled=True)
    capacity = gathered.shape[0]
    normed = normalize(gathered, norm_gain)
    block_count = lax.axis_size("blk")
    slot_load = slot_loads(span_len, span_owner, block_count)
    group_width = kv_weight.shape[3]
    local_groups = group_width // HD
    group_size = HEADS // KVH
    query_rows = queries.shape[1]
    query_grid = queries[0].reshape(query_rows, local_groups, group_size, HD)
    start_state = (
        jnp.full((query_rows, local_groups, group_size), -1e30, jnp.float32),
        jnp.zeros((query_rows, local_groups, group_size), jnp.float32),
        jnp.zeros((query_rows, local_groups, group_size, HD), jnp.float32),
    )
    projected = jnp.einsum(
        "cr,rtk->ctk",
        normed,
        lax.all_gather(kv_weight, "blk", axis=1, tiled=True)[0],
        preferred_element_type=jnp.float32,
    )
    key_rows = projected[:, 0].astype(jnp.bfloat16)
    value_rows = projected[:, 1].astype(jnp.bfloat16)
    final_state = attend(
        start_state,
        query_grid,
        lax.all_gather(key_rows, "blk", axis=0, tiled=True),
        lax.all_gather(value_rows, "blk", axis=0, tiled=True),
        slot_load,
        capacity,
    )
    denominator = final_state[1]
    numerator = final_state[2]
    attended = (numerator / denominator[..., None]).astype(jnp.bfloat16)
    return attended.reshape(1, query_rows, local_groups * group_size * HD)


def solution(mesh):
    in_specs = (
        P("section", "blk", "mp"),
        P(("blk", "section", "mp"), None),
        P(),
        P("section", "blk", None, "mp"),
        P(),
        P(),
    )
    out_specs = P("section", "blk", "mp")
    return jax.shard_map(local, mesh=mesh, in_specs=in_specs, out_specs=out_specs, check_vma=False)
```

profile of v0, /device:TPU:0, one launch (start us, length us, event | category | flops | bytes accessed | tf_op | source)
XLA Modules:
  0.0 140.6 jit_solution(526181429607966376)
XLA Ops:
  6.5 0.0 all-gather.4.cloned.1.call-start
  6.5 1.7 %copy.13 = bf16[1,256,2,256]{3,1,2,0:T(8,128)(2,1)} copy(bf16[1,256,2,256]{3,2,1,0:T(2,128)(2,1)} %param.9) | data formatting | bytes 524288 | tf_op args[3]
  8.2 0.0 all-gather.4.cloned.1.call-update
  8.2 1.1 copy.25
  9.4 7.5 %all_gather.12 = bf16[64,2048]{1,0:T(8,128)(2,1)S(1)} all-gather(bf16[16,2048]{1,0:T(8,128)(2,1)} %param.7), channel_id=1, replica_groups=mesh['section'=2,'blk'=8,'mp'=2] {'section','mp'}, dimensions={0}, use_global_device_ids=true | all-gather | bytes 327680 | tf_op jit(solution)/shard_map/all_gather | solution.py:60
  16.9 0.8 select_reduce_fusion.1
  17.6 0.1 select_reduce_fusion
  17.7 0.2 fusion.18
  17.9 43.4 %all-gather.4.cloned.1.call-done = bf16[1,2048,2,256]{3,1,2,0:T(8,128)(2,1)} async-done(((bf16[1,256,2,256]{3,1,2,0:T(8,128)(2,1)}), bf16[1,2048,2,256]{3,1,2,0:T(8,128)(2,1)}) %all-gather.4.cloned.1.call-update) | async-done | bytes 2097168 | tf_op jit(solution)/shard_map/all_gather | solution.py:78
  61.3 2.1 %fusion.13 = bf16[64,2,256]{2,0,1:T(8,128)(2,1)S(1)} fusion(bf16[1,2048,2,256]{3,1,2,0:T(8,128)(2,1)} %all-gather.4.cloned.1.call-done, bf16[64,2048]{1,0:T(8,128)(2,1)S(1)} %all_gather.12, f32[2048]{0:T(1024)} %param.8, f32[64]{0:T(128)S(1)} %add_rsqrt_fusion), kind=kOutput, calls=%fused_computation.13 | convolution fusion | flops 134774784 | bytes 2433280 | tf_op jit(solution)/shard_map/cr,rtk->ctk/dot_general | solution.py:75
  63.5 30.8 %all-gather.1 = bf16[512,1,256]{2,0,1:T(8,128)(2,1)S(1)} all-gather(bf16[64,1,256]{2,0,1:T(8,128)(2,1)S(1)} %get-tuple-element.5), channel_id=3, replica_groups=mesh['section'=2,'blk'=8,'mp'=2] {'blk'}, dimensions={0}, use_global_device_ids=true | all-gather | bytes 294912 | tf_op jit(solution)/shard_map/all_gather | solution.py:86
  94.3 0.1 reshape.41
  94.4 2.7 %bitcast_reduce_fusion = (f32[128,2,8]{0,2,1:T(8,128)S(1)}, f32[2,512,128,8]{2,1,3,0:T(8,128)}) fusion(pred[512]{0:T(512)(128)(4,1)S(1)} %fusion.28, bf16[128,2,8,128]{3,2,1,0:T(8,128)(2,1)S(1)} %bitcast.42, bf16[512,2,128,1]{2,1,0,3:T(2,128)(2,1)S(1)} %bitcast.43), kind=kOutput, calls=%fused_computation.1 | convolution fusion | flops 271579136 | bytes 4989440 | tf_op jit(solution)/shard_map/qgjd,rgd->qgjr/dot_general | solution.py:37
  97.1 30.8 %all-gather = bf16[512,1,256]{2,0,1:T(8,128)(2,1)S(1)} all-gather(bf16[64,1,256]{2,0,1:T(8,128)(2,1)S(1)} %get-tuple-element.6), channel_id=2, replica_groups=mesh['section'=2,'blk'=8,'mp'=2] {'blk'}, dimensions={0}, use_global_device_ids=true | all-gather | bytes 294912 | tf_op jit(solution)/shard_map/all_gather | solution.py:87
  127.9 0.1 copy.22
  128.0 0.0 copy-start
  128.0 3.4 %fusion.2 = f32[128,2,8]{0,2,1:T(8,128)S(1)} fusion(f32[2,512,128,8]{2,1,3,0:T(8,128)} %get-tuple-element.8, f32[128,2,8]{0,2,1:T(8,128)S(1)} %broadcast_maximum_fusion, pred[512]{0:T(512)(128)(4,1)S(1)} %fusion.28), kind=kLoop, calls=%fused_computation.5 | loop fusion | flops 5240832 | bytes 4211200 | tf_op jit(solution)/shard_map/reduce_sum | solution.py:43
  131.5 0.0 copy-done
  131.5 1.3 divide_convert_fusion
  132.8 1.0 copy.18
  (5 shorter events, 0.0 us)
Async XLA Ops:
  6.5 54.8 %all-gather.4.cloned.1.call-start = ((), (), s32[]{:S(2)}) async-start(), calls=%async_computation | async-start | bytes 2359296 | tf_op jit(solution)/shard_map/all_gather | solution.py:78
  128.0 3.5 %copy-start = (f32[2,512,128,8]{2,1,3,0:T(8,128)S(1)}, f32[2,512,128,8]{2,1,3,0:T(8,128)}, u32[]{:S(2)}) copy-start(f32[2,512,128,8]{2,1,3,0:T(8,128)} %get-tuple-element.8) | copy-start | bytes 12582916
Sparse Core Ops, SparseCore 0:
  9.5 51.7 all-gather.3
where the time goes:
time: 141 us
  blocking collectives  69.1 us (49%)
  waiting for transfers between devices  43.4 us (31%)
  between operations  13.5 us (10%)
  matrix products  6.14 us (4%)
  other arithmetic  4.49 us (3%)
  local copies, waits for them, and re-layouts  4.05 us (3%)
    all_gather x1, waiting for transfers between devices, local(): lax.all_gather(kv_weight, 'blk', axis=1, tiled=True)[0]  43.4 us
    all_gather x1, blocking collectives, local(): lax.all_gather(key_rows, 'blk', axis=0, tiled=True)  30.8 us
    all_gather x1, blocking collectives, local(): lax.all_gather(value_rows, 'blk', axis=0, tiled=True)  30.8 us
    all_gather x1, blocking collectives, local(): lax.all_gather(encoder_states, ('section', 'mp'), axis=0, tiled=True)  7.46 us
    reduce_sum x1, other arithmetic, attend_block(): denominator = jnp.sum(weights, axis=-1)  3.44 us
    unnamed x4, local copies, waits for them, and re-layouts  2.83 us
  transfers between devices with their start and end apart: 1, of which 1 were waited for; matrix products, arithmetic and copies ran while one was open for 2% of the time, Pallas kernels for 0%

commit v1 on v0

--- a/solution.py
+++ b/solution.py
@@ -6,6 +6,17 @@
 HEADS = 32
 KVH = 4
 HD = 128
+
+
+def collect(array, axis, dim):
+    ways = lax.axis_size(axis)
+    pieces = [array]
+    for far in range(1, ways):
+        pieces.append(
+            lax.ppermute(pieces[far - 1], axis, [(d, (d - 1) % ways) for d in range(ways)])
+        )
+    line = jnp.concatenate(pieces, axis=dim)
+    return jnp.roll(line, lax.axis_index(axis) * array.shape[dim], axis=dim)
 
 
 def normalize(states, norm_gain):
@@ -83,7 +94,7 @@
     final_state = attend(
         start_state,
         query_grid,
-        lax.all_gather(key_rows, "blk", axis=0, tiled=True),
+        collect(key_rows, "blk", 0),
         lax.all_gather(value_rows, "blk", axis=0, tiled=True),
         slot_load,
         capacity,

time: 141 us -> 144 us (1.021)
  blocking collectives: 69.1 us -> 38.3 us
  starting transfers between devices: 0.01 us -> 27.4 us
  waiting for transfers between devices: 43.4 us -> 54 us
  other arithmetic: 4.49 us -> 2.2 us
  matrix products: 6.14 us -> 4.49 us
    all_gather x1 -> x0, blocking collectives: 30.8 us -> none  [local(): lax.all_gather(key_rows, 'blk', axis=0, tiled=True)]
    ppermute x0 -> x7, starting transfers between devices: none -> 27.4 us  [collect(): lax.ppermute(pieces[far - 1], axis, [(d, (d - 1) % ways) for d in range(w...]
    ppermute x0 -> x7, waiting for transfers between devices: none -> 10.6 us  [collect(): lax.ppermute(pieces[far - 1], axis, [(d, (d - 1) % ways) for d in range(w...]
    reduce_sum x1, other arithmetic: 3.44 us -> 1.16 us  [attend_block(): denominator = jnp.sum(weights, axis=-1)]
    dot_general x1, matrix products: 2.74 us -> 1.09 us  [attend_block(): jnp.einsum('qgjd,rgd->qgjr', query_grid, key_grid, preferred_element_type...]
    unnamed x4 -> x17, local copies, waits for them, and re-layouts: 2.83 us -> 2.88 us
  transfers between devices with their start and end apart: 1 -> 8, of which waited for: 1 -> 7; matrix products, arithmetic and copies ran while one was open for 2% -> 2% of each run, Pallas kernels for 0% -> 0%
where the time goes in v1:
time: 144 us
  waiting for transfers between devices  54 us (38%)
  blocking collectives  38.3 us (27%)
  starting transfers between devices  27.4 us (19%)
  between operations  13.6 us (9%)
  matrix products  4.49 us (3%)
  local copies, waits for them, and re-layouts  4.21 us (3%)
  other arithmetic  2.2 us (2%)
    all_gather x1, waiting for transfers between devices, local(): lax.all_gather(kv_weight, 'blk', axis=1, tiled=True)[0]  43.4 us
    all_gather x1, blocking collectives, local(): lax.all_gather(value_rows, 'blk', axis=0, tiled=True)  30.8 us
    ppermute x7, starting transfers between devices, collect(): lax.ppermute(pieces[far - 1], axis, [(d, (d - 1) % ways) for d in range(w...  27.4 us
    ppermute x7, waiting for transfers between devices, collect(): lax.ppermute(pieces[far - 1], axis, [(d, (d - 1) % ways) for d in range(w...  10.6 us
    all_gather x1, blocking collectives, local(): lax.all_gather(encoder_states, ('section', 'mp'), axis=0, tiled=True)  7.46 us
    unnamed x17, local copies, waits for them, and re-layouts  2.88 us
  transfers between devices with their start and end apart: 8, of which 7 were waited for; matrix products, arithmetic and copies ran while one was open for 2% of the time, Pallas kernels for 0%

profile of v1, /device:TPU:0, one launch (start us, length us, event | category | flops | bytes accessed | tf_op | source)
XLA Modules:
  0.0 144.2 jit_solution(16578353406024057037)
XLA Ops:
  6.5 0.0 all-gather.3.cloned.1.call-start
  6.5 1.7 %copy.19 = bf16[1,256,2,256]{3,1,2,0:T(8,128)(2,1)} copy(bf16[1,256,2,256]{3,2,1,0:T(2,128)(2,1)} %param.9) | data formatting | bytes 524288 | tf_op args[3]
  8.2 0.0 all-gather.3.cloned.1.call-update
  8.3 1.1 copy.32
  9.4 7.5 %all_gather.9 = bf16[64,2048]{1,0:T(8,128)(2,1)S(1)} all-gather(bf16[16,2048]{1,0:T(8,128)(2,1)} %param.7), channel_id=1, replica_groups=mesh['section'=2,'blk'=8,'mp'=2] {'section','mp'}, dimensions={0}, use_global_device_ids=true | all-gather | bytes 327680 | tf_op jit(solution)/shard_map/all_gather | solution.py:71
  16.9 0.8 select_reduce_fusion.1
  17.7 0.1 select_reduce_fusion
  17.8 0.2 fusion.18
  17.9 43.4 %all-gather.3.cloned.1.call-done = bf16[1,2048,2,256]{3,1,2,0:T(8,128)(2,1)} async-done(((bf16[1,256,2,256]{3,1,2,0:T(8,128)(2,1)}), bf16[1,2048,2,256]{3,1,2,0:T(8,128)(2,1)}) %all-gather.3.cloned.1.call-update) | async-done | bytes 2097168 | tf_op jit(solution)/shard_map/all_gather | solution.py:89
  61.3 2.1 %fusion.13 = bf16[64,2,256]{2,0,1:T(8,128)(2,1)S(1)} fusion(bf16[1,2048,2,256]{3,1,2,0:T(8,128)(2,1)} %all-gather.3.cloned.1.call-done, bf16[64,2048]{1,0:T(8,128)(2,1)S(1)} %all_gather.9, f32[2048]{0:T(1024)} %param.8, f32[64]{0:T(128)S(1)} %add_rsqrt_fusion), kind=kOutput, calls=%fused_computation.13 | convolution fusion | flops 134774784 | bytes 2433280 | tf_op jit(solution)/shard_map/cr,rtk->ctk/dot_general | solution.py:86
  63.5 1.9 %collective-permute-start = (bf16[64,256]{1,0:T(8,128)(2,1)S(1)}, bf16[64,256]{1,0:T(8,128)(2,1)S(1)}, u32[]{:S(2)}, u32[]{:S(2)}) collective-permute-start(bf16[64,256]{1,0:T(8,128)(2,1)S(1)} %get-tuple-element.5), channel_id=1, source_target_pairs={{0,14},{2,0},{4,2},{6,4},{8,6},{10,8},{12,10},{14,12},{1,15},{3,1}... | collective-permute-start | bytes 98312 | tf_op jit(solution)/shard_map/ppermute | solution.py:16
  65.4 30.8 %all-gather = bf16[512,1,256]{2,0,1:T(8,128)(2,1)S(1)} all-gather(bf16[64,1,256]{2,0,1:T(8,128)(2,1)S(1)} %get-tuple-element.6), channel_id=2, replica_groups=mesh['section'=2,'blk'=8,'mp'=2] {'blk'}, dimensions={0}, use_global_device_ids=true | all-gather | bytes 294912 | tf_op jit(solution)/shard_map/all_gather | solution.py:98
  96.2 0.1 copy.29
  96.4 0.0 collective-permute-done
  96.4 1.4 %collective-permute-start.1 = (bf16[64,256]{1,0:T(8,128)(2,1)S(1)}, bf16[64,256]{1,0:T(8,128)(2,1)S(1)}, u32[]{:S(2)}, u32[]{:S(2)}) collective-permute-start(bf16[64,256]{1,0:T(8,128)(2,1)S(1)} %collective-permute-done), channel_id=1, source_target_pairs={{0,14},{2,0},{4,2},{6,4},{8,6},{10,8},{12,10},{14,12},{1,15},{3,1}... | collective-permute-start | bytes 98312 | tf_op jit(solution)/shard_map/ppermute | solution.py:16
  97.8 2.6 %collective-permute-done.1 = bf16[64,256]{1,0:T(8,128)(2,1)S(1)} collective-permute-done((bf16[64,256]{1,0:T(8,128)(2,1)S(1)}, bf16[64,256]{1,0:T(8,128)(2,1)S(1)}, u32[]{:S(2)}, u32[]{:S(2)}) %collective-permute-start.1) | collective-permute-done | bytes 32800 | tf_op jit(solution)/shard_map/ppermute | solution.py:16
  100.4 4.0 %collective-permute-start.2 = (bf16[64,256]{1,0:T(8,128)(2,1)S(1)}, bf16[64,256]{1,0:T(8,128)(2,1)S(1)}, u32[]{:S(2)}, u32[]{:S(2)}) collective-permute-start(bf16[64,256]{1,0:T(8,128)(2,1)S(1)} %collective-permute-done.1), channel_id=1, source_target_pairs={{0,14},{2,0},{4,2},{6,4},{8,6},{10,8},{12,10},{14,12},{1,15},{3,1}... | collective-permute-start | bytes 98312 | tf_op jit(solution)/shard_map/ppermute | solution.py:16
  104.4 1.6 %collective-permute-done.2 = bf16[64,256]{1,0:T(8,128)(2,1)S(1)} collective-permute-done((bf16[64,256]{1,0:T(8,128)(2,1)S(1)}, bf16[64,256]{1,0:T(8,128)(2,1)S(1)}, u32[]{:S(2)}, u32[]{:S(2)}) %collective-permute-start.2) | collective-permute-done | bytes 32800 | tf_op jit(solution)/shard_map/ppermute | solution.py:16
  106.0 5.0 %collective-permute-start.3 = (bf16[64,256]{1,0:T(8,128)(2,1)S(1)}, bf16[64,256]{1,0:T(8,128)(2,1)S(1)}, u32[]{:S(2)}, u32[]{:S(2)}) collective-permute-start(bf16[64,256]{1,0:T(8,128)(2,1)S(1)} %collective-permute-done.2), channel_id=1, source_target_pairs={{0,14},{2,0},{4,2},{6,4},{8,6},{10,8},{12,10},{14,12},{1,15},{3,1}... | collective-permute-start | bytes 98312 | tf_op jit(solution)/shard_map/ppermute | solution.py:16
  111.0 1.6 %collective-permute-done.3 = bf16[64,256]{1,0:T(8,128)(2,1)S(1)} collective-permute-done((bf16[64,256]{1,0:T(8,128)(2,1)S(1)}, bf16[64,256]{1,0:T(8,128)(2,1)S(1)}, u32[]{:S(2)}, u32[]{:S(2)}) %collective-permute-start.3) | collective-permute-done | bytes 32800 | tf_op jit(solution)/shard_map/ppermute | solution.py:16
  112.6 5.0 %collective-permute-start.4 = (bf16[64,256]{1,0:T(8,128)(2,1)S(1)}, bf16[64,256]{1,0:T(8,128)(2,1)S(1)}, u32[]{:S(2)}, u32[]{:S(2)}) collective-permute-start(bf16[64,256]{1,0:T(8,128)(2,1)S(1)} %collective-permute-done.3), channel_id=1, source_target_pairs={{0,14},{2,0},{4,2},{6,4},{8,6},{10,8},{12,10},{14,12},{1,15},{3,1}... | collective-permute-start | bytes 98312 | tf_op jit(solution)/shard_map/ppermute | solution.py:16
  117.7 1.6 %collective-permute-done.4 = bf16[64,256]{1,0:T(8,128)(2,1)S(1)} collective-permute-done((bf16[64,256]{1,0:T(8,128)(2,1)S(1)}, bf16[64,256]{1,0:T(8,128)(2,1)S(1)}, u32[]{:S(2)}, u32[]{:S(2)}) %collective-permute-start.4) | collective-permute-done | bytes 32800 | tf_op jit(solution)/shard_map/ppermute | solution.py:16
  119.3 5.0 %collective-permute-start.5 = (bf16[64,256]{1,0:T(8,128)(2,1)S(1)}, bf16[64,256]{1,0:T(8,128)(2,1)S(1)}, u32[]{:S(2)}, u32[]{:S(2)}) collective-permute-start(bf16[64,256]{1,0:T(8,128)(2,1)S(1)} %collective-permute-done.4), channel_id=1, source_target_pairs={{0,14},{2,0},{4,2},{6,4},{8,6},{10,8},{12,10},{14,12},{1,15},{3,1}... | collective-permute-start | bytes 98312 | tf_op jit(solution)/shard_map/ppermute | solution.py:16
  124.3 1.6 %collective-permute-done.5 = bf16[64,256]{1,0:T(8,128)(2,1)S(1)} collective-permute-done((bf16[64,256]{1,0:T(8,128)(2,1)S(1)}, bf16[64,256]{1,0:T(8,128)(2,1)S(1)}, u32[]{:S(2)}, u32[]{:S(2)}) %collective-permute-start.5) | collective-permute-done | bytes 32800 | tf_op jit(solution)/shard_map/ppermute | solution.py:16
  125.9 5.0 %collective-permute-start.6 = (bf16[64,256]{1,0:T(8,128)(2,1)S(1)}, bf16[64,256]{1,0:T(8,128)(2,1)S(1)}, u32[]{:S(2)}, u32[]{:S(2)}) collective-permute-start(bf16[64,256]{1,0:T(8,128)(2,1)S(1)} %collective-permute-done.5), channel_id=1, source_target_pairs={{0,14},{2,0},{4,2},{6,4},{8,6},{10,8},{12,10},{14,12},{1,15},{3,1}... | collective-permute-start | bytes 98312 | tf_op jit(solution)/shard_map/ppermute | solution.py:16
  130.9 1.6 %collective-permute-done.6 = bf16[64,256]{1,0:T(8,128)(2,1)S(1)} collective-permute-done((bf16[64,256]{1,0:T(8,128)(2,1)S(1)}, bf16[64,256]{1,0:T(8,128)(2,1)S(1)}, u32[]{:S(2)}, u32[]{:S(2)}) %collective-permute-start.6) | collective-permute-done | bytes 32800 | tf_op jit(solution)/shard_map/ppermute | solution.py:16
  132.6 0.1 copy.20
  132.7 1.1 bitcast_reduce_fusion
  133.9 1.2 fusion.2
  135.0 1.3 divide_convert_fusion
  136.3 1.0 copy.25
  (22 shorter events, 0.1 us)
Async XLA Ops:
  6.5 54.8 %all-gather.3.cloned.1.call-start = ((), (), s32[]{:S(2)}) async-start(), calls=%async_computation | async-start | bytes 2359296 | tf_op jit(solution)/shard_map/all_gather | solution.py:89
  63.5 32.9 %collective-permute-start = (bf16[64,256]{1,0:T(8,128)(2,1)S(1)}, bf16[64,256]{1,0:T(8,128)(2,1)S(1)}, u32[]{:S(2)}, u32[]{:S(2)}) collective-permute-start(bf16[64,256]{1,0:T(8,128)(2,1)S(1)} %get-tuple-element.5), channel_id=1, source_target_pairs={{0,14},{2,0},{4,2},{6,4},{8,6},{10,8},{12,10},{14,12},{1,15},{3,1}... | collective-permute-start | bytes 98312 | tf_op jit(solution)/shard_map/ppermute | solution.py:16
  96.4 4.0 %collective-permute-start.1 = (bf16[64,256]{1,0:T(8,128)(2,1)S(1)}, bf16[64,256]{1,0:T(8,128)(2,1)S(1)}, u32[]{:S(2)}, u32[]{:S(2)}) collective-permute-start(bf16[64,256]{1,0:T(8,128)(2,1)S(1)} %collective-permute-done), channel_id=1, source_target_pairs={{0,14},{2,0},{4,2},{6,4},{8,6},{10,8},{12,10},{14,12},{1,15},{3,1}... | collective-permute-start | bytes 98312 | tf_op jit(solution)/shard_map/ppermute | solution.py:16
  100.4 5.6 %collective-permute-start.2 = (bf16[64,256]{1,0:T(8,128)(2,1)S(1)}, bf16[64,256]{1,0:T(8,128)(2,1)S(1)}, u32[]{:S(2)}, u32[]{:S(2)}) collective-permute-start(bf16[64,256]{1,0:T(8,128)(2,1)S(1)} %collective-permute-done.1), channel_id=1, source_target_pairs={{0,14},{2,0},{4,2},{6,4},{8,6},{10,8},{12,10},{14,12},{1,15},{3,1}... | collective-permute-start | bytes 98312 | tf_op jit(solution)/shard_map/ppermute | solution.py:16
  106.0 6.6 %collective-permute-start.3 = (bf16[64,256]{1,0:T(8,128)(2,1)S(1)}, bf16[64,256]{1,0:T(8,128)(2,1)S(1)}, u32[]{:S(2)}, u32[]{:S(2)}) collective-permute-start(bf16[64,256]{1,0:T(8,128)(2,1)S(1)} %collective-permute-done.2), channel_id=1, source_target_pairs={{0,14},{2,0},{4,2},{6,4},{8,6},{10,8},{12,10},{14,12},{1,15},{3,1}... | collective-permute-start | bytes 98312 | tf_op jit(solution)/shard_map/ppermute | solution.py:16
  112.6 6.6 %collective-permute-start.4 = (bf16[64,256]{1,0:T(8,128)(2,1)S(1)}, bf16[64,256]{1,0:T(8,128)(2,1)S(1)}, u32[]{:S(2)}, u32[]{:S(2)}) collective-permute-start(bf16[64,256]{1,0:T(8,128)(2,1)S(1)} %collective-permute-done.3), channel_id=1, source_target_pairs={{0,14},{2,0},{4,2},{6,4},{8,6},{10,8},{12,10},{14,12},{1,15},{3,1}... | collective-permute-start | bytes 98312 | tf_op jit(solution)/shard_map/ppermute | solution.py:16
  119.3 6.6 %collective-permute-start.5 = (bf16[64,256]{1,0:T(8,128)(2,1)S(1)}, bf16[64,256]{1,0:T(8,128)(2,1)S(1)}, u32[]{:S(2)}, u32[]{:S(2)}) collective-permute-start(bf16[64,256]{1,0:T(8,128)(2,1)S(1)} %collective-permute-done.4), channel_id=1, source_target_pairs={{0,14},{2,0},{4,2},{6,4},{8,6},{10,8},{12,10},{14,12},{1,15},{3,1}... | collective-permute-start | bytes 98312 | tf_op jit(solution)/shard_map/ppermute | solution.py:16
  125.9 6.6 %collective-permute-start.6 = (bf16[64,256]{1,0:T(8,128)(2,1)S(1)}, bf16[64,256]{1,0:T(8,128)(2,1)S(1)}, u32[]{:S(2)}, u32[]{:S(2)}) collective-permute-start(bf16[64,256]{1,0:T(8,128)(2,1)S(1)} %collective-permute-done.5), channel_id=1, source_target_pairs={{0,14},{2,0},{4,2},{6,4},{8,6},{10,8},{12,10},{14,12},{1,15},{3,1}... | collective-permute-start | bytes 98312 | tf_op jit(solution)/shard_map/ppermute | solution.py:16
Sparse Core Ops, SparseCore 0:
  9.5 51.7 all-gather.2
